TPU v7x, 32 devices: a whole 2x2x4 slice. The times are simulated.
32 devices in a mesh: seq: 16 (over z, y, x), mdl: 2 (over core).
Axes of the slice: x: 2, y: 2, z: 4, core: 2. Of those that a mesh axis runs over, the one named last changes fastest.
Arguments:
- hidden_in: bfloat16 [32, 4, 2048], P(None, None, 'seq'), may hold values from -25 to 25
- cache_keys: bfloat16 [32, 512, 2048], P(None, 'seq', 'mdl'), may hold values from -250 to 250, as said below
- cache_values: bfloat16 [32, 512, 2048], P(None, 'seq', 'mdl'), may hold values from -6 to 6
- lengths: int32 [32], replicated, may hold values from 1 to 508, as said below
- query_weight: bfloat16 [2048, 2048], P('seq', 'mdl'), may hold values from -0.125 to 0.125
- key_weight: bfloat16 [2048, 2048], P('seq', 'mdl'), may hold values from -0.125 to 0.125
- value_weight: bfloat16 [2048, 2048], P('seq', 'mdl'), may hold values from -0.125 to 0.125
- out_weight: bfloat16 [2048, 2048], P('mdl', 'seq'), may hold values from -0.125 to 0.125
- gate_weight: bfloat16 [2048, 8192], P('seq', 'mdl'), may hold values from -0.125 to 0.125
- up_weight: bfloat16 [2048, 8192], P('seq', 'mdl'), may hold values from -0.125 to 0.125
- down_weight: bfloat16 [8192, 2048], P('mdl', 'seq'), may hold values from -0.0625 to 0.0625
Outputs:
- hidden_out: bfloat16 [32, 4, 2048], P(None, None, 'seq')
- new_cache_keys: bfloat16 [32, 512, 2048], P(None, 'seq', 'mdl')
- new_cache_values: bfloat16 [32, 512, 2048], P(None, 'seq', 'mdl')
Inputs may be any that keep to these rules, and one draw needn't show every extreme that they name: `cache_keys`: keys are stored after their rotary embedding. `lengths`: at least one request has exactly 508 cached positions.
All inputs are finite; a program needn't handle non-finite values.
Results may differ from a plain program's by a relative error of at most 0.012.
The roundings to bfloat16 on the way count: a program that leaves them out, or rounds other values in their place, can miss the bound.
Values may be sent and summed in bfloat16 or wider, within the bound.
A program may use at most 64 MiB of HBM per device.

v0:
```python
import math
import jax
import jax.numpy as jnp
from jax import lax
from jax.sharding import PartitionSpec as P

D = 2048
HEADS = 16
EPS = 1e-05
THETA = 10000.0
NEGATIVE = -1e30


def rotate(vectors, placed_pos):
    head_size = vectors.shape[-1]
    half_dim = head_size // 2
    freqs = THETA ** (-jnp.arange(half_dim, dtype=jnp.float32) * 2.0 / head_size)
    angles = placed_pos.astype(jnp.float32)[..., None, None] * freqs
    cosine = jnp.cos(angles)
    sine = jnp.sin(angles)
    first_half = vectors[..., :half_dim]
    second_half = vectors[..., half_dim:]
    return jnp.concatenate(
        [first_half * cosine - second_half * sine, second_half * cosine + first_half * sine],
        axis=-1,
    )


def normalize(widened, row_sums, square_sums):
    row_mean = row_sums / D
    second_moment = square_sums / D
    inverse = 1.0 / jnp.sqrt(second_moment - row_mean * row_mean + EPS)
    return ((widened - row_mean[..., None]) * inverse[..., None]).astype(jnp.bfloat16)


def body(
    hidden_in,
    cache_keys,
    cache_values,
    lengths,
    query_weight,
    key_weight,
    value_weight,
    out_weight,
    gate_weight,
    up_weight,
    down_weight,
):
    requests, token_count, narrow_width = hidden_in.shape
    slot_count = cache_keys.shape[1]
    local_width = cache_keys.shape[2]
    head_size = D // HEADS
    local_heads = local_width // head_size
    score_scale = 1.0 / math.sqrt(head_size)
    shard_index = lax.axis_index("seq")
    slot_ids = shard_index * slot_count + jnp.arange(slot_count, dtype=jnp.int32)
    live_slots = slot_ids[None, :] < lengths[:, None]
    old_keys = cache_keys.reshape(requests, slot_count, local_heads, head_size)
    old_values = cache_values.reshape(requests, slot_count, local_heads, head_size).astype(
        jnp.float32
    )
    positions = lengths[:, None] + jnp.arange(token_count, dtype=jnp.int32)[None, :]
    out_list = []
    key_list = []
    value_list = []
    for token_step in range(token_count):
        row_block = hidden_in[:, token_step : token_step + 1]
        block_rows = row_block.shape[1]
        widened = row_block.astype(jnp.float32)
        row_sums, square_sums = lax.psum(
            (jnp.sum(widened, axis=-1), jnp.sum(widened * widened, axis=-1)), "seq"
        )
        normed = normalize(widened, row_sums, square_sums)
        query_part = jnp.einsum(
            "rnc,cm->rnm", normed, query_weight, preferred_element_type=jnp.float32
        )
        key_part = jnp.einsum("rnc,cm->rnm", normed, key_weight, preferred_element_type=jnp.float32)
        value_part = jnp.einsum(
            "rnc,cm->rnm", normed, value_weight, preferred_element_type=jnp.float32
        )
        queries, keys_full, values_full = lax.psum((query_part, key_part, value_part), "seq")
        placed_pos = positions[:, token_step : token_step + block_rows]
        queries = rotate(
            queries.reshape(requests, block_rows, local_heads, head_size), placed_pos
        ).astype(jnp.bfloat16)
        new_key = rotate(
            keys_full.reshape(requests, block_rows, local_heads, head_size), placed_pos
        ).astype(jnp.bfloat16)
        new_value = values_full.reshape(requests, block_rows, local_heads, head_size).astype(
            jnp.bfloat16
        )
        keys_new = jnp.concatenate(key_list + [new_key], axis=1)
        values_new = jnp.concatenate(value_list + [new_value], axis=1)
        old_scores = (
            jnp.einsum("rnhd,rjhd->rnhj", queries, old_keys, preferred_element_type=jnp.float32)
            * score_scale
        )
        old_scores = jnp.where(live_slots[:, None, None, :], old_scores, NEGATIVE)
        top_old = jnp.max(old_scores, axis=-1)
        weights_old = jnp.where(
            live_slots[:, None, None, :], jnp.exp(old_scores - top_old[..., None]), 0.0
        )
        total_old = jnp.sum(weights_old, axis=-1)
        summed_old = jnp.einsum(
            "rnhj,rjhd->rnhd", weights_old, old_values, precision=lax.Precision.HIGHEST
        )
        top_cache = lax.pmax(top_old, "seq")
        factor_old = jnp.exp(top_old - top_cache)
        total_cache, summed_cache = lax.psum(
            (total_old * factor_old, summed_old * factor_old[..., None]), "seq"
        )
        new_scores = (
            jnp.einsum("rnhd,rshd->rnhs", queries, keys_new, preferred_element_type=jnp.float32)
            * score_scale
        )
        key_index = jnp.arange(keys_new.shape[1], dtype=jnp.int32)
        query_index = token_step + jnp.arange(block_rows, dtype=jnp.int32)
        allowed = key_index[None, :] <= query_index[:, None]
        new_scores = jnp.where(allowed[None, :, None, :], new_scores, NEGATIVE)
        top_new = jnp.max(new_scores, axis=-1)
        weights_new = jnp.exp(new_scores - top_new[..., None])
        total_new = jnp.sum(weights_new, axis=-1)
        summed_new = jnp.einsum(
            "rnhs,rshd->rnhd",
            weights_new,
            values_new.astype(jnp.float32),
            precision=lax.Precision.HIGHEST,
        )
        top_score = jnp.maximum(top_cache, top_new)
        factor_cache = jnp.exp(top_cache - top_score)
        factor_new = jnp.exp(top_new - top_score)
        running = total_cache * factor_cache + total_new * factor_new
        combined = summed_cache * factor_cache[..., None] + summed_new * factor_new[..., None]
        attended = (
            (combined / running[..., None])
            .astype(jnp.bfloat16)
            .reshape(requests, block_rows, local_width)
        )
        attn_part = jnp.einsum(
            "rnm,mc->rnc", attended, out_weight, preferred_element_type=jnp.float32
        )
        mixed = widened + lax.psum(attn_part, "mdl")
        sums_mixed, squares_mixed = lax.psum(
            (jnp.sum(mixed, axis=-1), jnp.sum(mixed * mixed, axis=-1)), "seq"
        )
        normed2 = normalize(mixed, sums_mixed, squares_mixed)
        gate_part = jnp.einsum(
            "rnc,cf->rnf", normed2, gate_weight, preferred_element_type=jnp.float32
        )
        up_part = jnp.einsum("rnc,cf->rnf", normed2, up_weight, preferred_element_type=jnp.float32)
        gate_full, up_full = lax.psum((gate_part, up_part), "seq")
        act_full = (jax.nn.silu(gate_full) * up_full).astype(jnp.bfloat16)
        down_part = jnp.einsum(
            "rnf,fc->rnc", act_full, down_weight, preferred_element_type=jnp.float32
        )
        block_out = (mixed + lax.psum(down_part, "mdl")).astype(jnp.bfloat16)
        block_out, new_key, new_value = (block_out, new_key, new_value)
        out_list.append(block_out)
        key_list.append(new_key)
        value_list.append(new_value)
    hidden_out = jnp.concatenate(out_list, axis=1)
    keys_all = jnp.concatenate(key_list, axis=1)
    values_all = jnp.concatenate(value_list, axis=1)
    slot_hits = slot_ids[None, None, :] == positions[:, :, None]
    one_hot = slot_hits.astype(jnp.bfloat16)
    written = jnp.any(slot_hits, axis=1)[..., None]
    placed_keys = jnp.einsum(
        "rts,rtm->rsm",
        one_hot,
        keys_all.reshape(requests, token_count, local_width),
        preferred_element_type=jnp.float32,
    ).astype(jnp.bfloat16)
    placed_values = jnp.einsum(
        "rts,rtm->rsm",
        one_hot,
        values_all.reshape(requests, token_count, local_width),
        preferred_element_type=jnp.float32,
    ).astype(jnp.bfloat16)
    new_cache_keys = jnp.where(written, placed_keys, cache_keys)
    new_cache_values = jnp.where(written, placed_values, cache_values)
    return (hidden_out, new_cache_keys, new_cache_values)


def solution(mesh):
    placed = (
        P(None, None, "seq"),
        P(None, "seq", "mdl"),
        P(None, "seq", "mdl"),
        P(),
        P("seq", "mdl"),
        P("seq", "mdl"),
        P("seq", "mdl"),
        P("mdl", "seq"),
        P("seq", "mdl"),
        P("seq", "mdl"),
        P("mdl", "seq"),
    )
    return jax.shard_map(
        body,
        mesh=mesh,
        in_specs=placed,
        out_specs=(P(None, None, "seq"), P(None, "seq", "mdl"), P(None, "seq", "mdl")),
        check_vma=False,
    )
```

profile of v0, /device:TPU:0, one launch (start us, length us, event | category | flops | bytes accessed | tf_op | source)
XLA Modules:
  0.0 663.0 jit_solution(5343042440964158596)
XLA Ops:
  8.5 43.5 %all-reduce.2 = (f32[32,1]{0,1:T(1,128)S(1)}, f32[32,1]{0,1:T(1,128)S(1)}, f32[32,1]{0,1:T(1,128)S(1)}, f32[32,1]{0,1:T(1,128)S(1)}, f32[32,1]{0,1:T(1,128)S(1)}...) all-reduce(f32[32,1]{0,1:T(1,128)S(1)} %bitcast.640, ...), channel_id=1, replica_groups=mesh['seq'=16,'mdl'=2] {'seq'}, use_global_device_ids=true, to_apply=%region_67.68 | all-reduce | flops 256 | bytes 2048 | tf_op jit(solution)/shard_map/psum | solution.py:70
  52.0 1.2 convolution_bitcast_fusion.10
  53.9 1.2 convolution_bitcast_fusion.19
  55.8 1.2 convolution_bitcast_fusion.16
  63.4 100.4 %all-reduce.20.cloned.1.call-done = (f32[32,1,8,128]{3,2,0,1:T(8,128)}, f32[32,1,8,128]{3,2,0,1:T(8,128)}, f32[32,1,8,128]{3,2,0,1:T(8,128)}, f32[32,1,8,128]{3,2,0,1:T(8,128)}) async-done(((f32[32,1,8,128]{3,2,0,1:T(8,128)}, f32[32,1,8,128]{3,2,0,1:T(8,128)}, f32[32,1,8,128]{3,2,0,1:T(8,128)}, f32[32,1,8,128]{3,2,0,1:T(8,128)}), (f32[32,1,8,128]{3,2,0,1:T(8,128)}, f32[32,1,8,128]{3,2,0,1:T(8,128)}, ...) | async-done | bytes 524304 | tf_op jit(solution)/shard_map/psum | solution.py:81
  163.8 1.2 fusion.71
  165.2 2.8 fusion.14
  168.2 1.2 fusion.12
  169.6 1.2 fusion.10
  171.0 1.2 fusion.8
  172.9 1.8 fusion
  174.6 1.8 fusion.2
  176.4 1.8 fusion.4
  178.2 1.8 fusion.6
  179.9 75.1 %all-reduce.6 = (f32[32,1,8]{2,0,1:T(8,128)S(1)}, f32[32,1,8]{2,0,1:T(8,128)S(1)}, f32[32,1,8]{2,0,1:T(8,128)S(1)}, f32[32,1,8]{2,0,1:T(8,128)S(1)}) all-reduce(f32[32,1,8]{2,0,1:T(8,128)S(1)} %bitcast.619, f32[32,1,8]{2,0,1:T(8,128)S(1)} %bitcast.618, f32[32,1,8]{2,0,1:T(8,128)S(1)} %bitcast.617, ...), channel_id=1, replica_groups=mesh['seq'=16,'mdl'=2] {'seq'}, use_global_device_ids=true, to_apply=%region_70.71 | all-reduce | flops 1024 | bytes 8192 | tf_op jit(solution)/shard_map/pmax | solution.py:107
  258.4 81.7 %all-reduce.25 = (bf16[32,1,1024]{2,0,1:T(8,128)(2,1)S(1)}, bf16[32,1,1024]{2,0,1:T(8,128)(2,1)S(1)}, bf16[32,1,1024]{2,0,1:T(8,128)(2,1)S(1)}, bf16[32,1,1024]{...) all-reduce(f32[32,1,1024]{2,0,1:T(8,128)S(1)} %convolution_bitcast_, ...), channel_id=1, replica_groups=mesh['seq'=16,'mdl'=2] {'seq'}, use_global_device_ids=true, to_apply=%region_74.75 | all-reduce | flops 132096 | bytes 794624 | tf_op jit(solution)/shard_map/psum | solution.py:81
  340.5 29.7 %all-reduce.18.cloned.1.call-done = (f32[32,1,8,128]{3,2,0,1:T(8,128)}, f32[32,1,8,128]{3,2,0,1:T(8,128)}, f32[32,1,8,128]{3,2,0,1:T(8,128)}, f32[32,1,8,128]{3,...) async-done(((f32[32,1,8,128]{3,2,0,1:T(8,128)}, f32[32,1,8,128]{3,2,0,1:T(8,128)}, ...) | async-done | bytes 1048592 | tf_op jit(solution)/shard_map/psum | solution.py:81
  390.5 17.2 %all-reduce.24.cloned.1.call-done = (f32[32,1,128]{2,0,1:T(8,128)}, f32[32,1,128]{2,0,1:T(8,128)}, f32[32,1,128]{2,0,1:T(8,128)}, f32[32,1,128]{2,0,1:T(8,128)}) async-done(((f32[32,1,128]{2,0,1:T(8,128)}, f32[32,1,128]{2,0,1:T(8,128)}, f32[32,1,128]{2,0,1:T(8,128)}, f32[32,1,128]{2,0,1:T(8,128)}), (f32[32,1,128]{2,0,1:T(8,128)}, f32[32,1,128]{2,0,1:T(8,128)}, f32[32,1,128]{2,0,1:T(8,128)}, ...) | async-done | bytes 65552 | tf_op jit(solution)/shard_map/psum | solution.py:142
  411.0 42.0 %all-reduce = (f32[32,1]{0,1:T(1,128)S(1)}, f32[32,1]{0,1:T(1,128)S(1)}, f32[32,1]{0,1:T(1,128)S(1)}, f32[32,1]{0,1:T(1,128)S(1)}, f32[32,1]{0,1:T(1,128)S(1)}, ...) all-reduce(f32[32,1]{0,1:T(1,128)S(1)} %bitcast.648, ...), channel_id=1, replica_groups=mesh['seq'=16,'mdl'=2] {'seq'}, use_global_device_ids=true, to_apply=%region_82.83 | all-reduce | flops 256 | bytes 2048 | tf_op jit(solution)/shard_map/psum | solution.py:143
  465.7 3.3 convert_select_fusion
  469.1 161.2 %all-reduce.16.cloned.1.call-done = (f32[32,1,4096]{2,0,1:T(8,128)}, f32[32,1,4096]{2,0,1:T(8,128)}, f32[32,1,4096]{2,0,1:T(8,128)}, f32[32,1,4096]{2,0,1:T(8,12...) async-done(((f32[32,1,4096]{2,0,1:T(8,128)}, f32[32,1,4096]{2,0,1:T(8,128)}, f32[32,1,4096]{2,0,1:T(8,128)}, ...) | async-done | bytes 4194320 | tf_op jit(solution)/shard_map/psum | solution.py:151
  630.3 2.6 convolution_bitcast_fusion.20
  636.1 3.7 convert_select_fusion.1
  639.7 13.2 %all-reduce.22.cloned.1.call-done = (f32[32,1,128]{2,0,1:T(8,128)}, f32[32,1,128]{2,0,1:T(8,128)}, f32[32,1,128]{2,0,1:T(8,128)}, f32[32,1,128]{2,0,1:T(8,128)}) async-done(((f32[32,1,128]{2,0,1:T(8,128)}, f32[32,1,128]{2,0,1:T(8,128)}, f32[32,1,128]{2,0,1:T(8,128)}, f32[32,1,128]{2,0,1:T(8,128)}), (f32[32,1,128]{2,0,1:T(8,128)}, f32[32,1,128]{2,0,1:T(8,128)}, f32[32,1,128]{2,0,1:T(8,128)}, ...) | async-done | bytes 65552 | tf_op jit(solution)/shard_map/psum | solution.py:156
  (246 shorter events, 56.8 us)
Async XLA Ops:
  7.2 446.6 %copy-start = (bf16[128,4096]{1,0:T(8,128)(2,1)S(1)}, bf16[128,4096]{1,0:T(8,128)(2,1)}, u32[]{:S(2)}) copy-start(bf16[128,4096]{1,0:T(8,128)(2,1)} %param.20) | copy-start | bytes 3145732
  7.2 50.5 %copy-start.2 = (bf16[128,1024]{1,0:T(8,128)(2,1)S(1)}, bf16[128,1024]{1,0:T(8,128)(2,1)}, u32[]{:S(2)}) copy-start(bf16[128,1024]{1,0:T(8,128)(2,1)} %param.15) | copy-start | bytes 786436
  7.2 51.5 %copy-start.3 = (bf16[128,1024]{1,0:T(8,128)(2,1)S(1)}, bf16[128,1024]{1,0:T(8,128)(2,1)}, u32[]{:S(2)}) copy-start(bf16[128,1024]{1,0:T(8,128)(2,1)} %param.16) | copy-start | bytes 786436
  7.2 156.6 %all-reduce.20.cloned.1.call-start = ((), (), s32[]{:S(2)}) async-start(), calls=%async_computation.2 | async-start | bytes 1048576 | tf_op jit(solution)/shard_map/psum | solution.py:81
  58.6 311.6 %all-reduce.18.cloned.1.call-start = ((), (), s32[]{:S(2)}) async-start(), calls=%async_computation.1 | async-start | bytes 2097152 | tf_op jit(solution)/shard_map/psum | solution.py:81
  62.9 102.1 %copy-start.32 = (s32[32,4]{0,1:T(4,128)}, s32[32,4]{0,1:T(4,128)S(1)}, u32[]{:S(2)}) copy-start(s32[32,4]{0,1:T(4,128)S(1)} %iota_add_fusion) | copy-start | bytes 1540
  63.0 102.1 %copy-start.35 = (s32[32]{0:T(128)}, s32[32]{0:T(128)S(1)}, u32[]{:S(2)}) copy-start(s32[32]{0:T(128)S(1)} %iota_add_fusion.1) | copy-start | bytes 388
  258.1 149.5 %all-reduce.24.cloned.1.call-start = ((), (), s32[]{:S(2)}) async-start(), calls=%async_computation.4 | async-start | bytes 131072 | tf_op jit(solution)/shard_map/psum | solution.py:142
  340.2 34.7 %copy-start.11 = (bf16[32,1,1024]{2,0,1:T(8,128)(2,1)}, bf16[32,1,1024]{2,0,1:T(8,128)(2,1)S(1)}, u32[]{:S(2)}) copy-start(bf16[32,1,1024]{2,0,1:T(8,128)(2,1)S(1)} %get-tuple-element.40) | copy-start | bytes 196612
  340.2 34.7 %copy-start.12 = (bf16[32,1,1024]{2,0,1:T(8,128)(2,1)}, bf16[32,1,1024]{2,0,1:T(8,128)(2,1)S(1)}, u32[]{:S(2)}) copy-start(bf16[32,1,1024]{2,0,1:T(8,128)(2,1)S(1)} %get-tuple-element.41) | copy-start | bytes 196612
  340.2 43.5 %copy-start.13 = (bf16[32,1,1024]{2,0,1:T(8,128)(2,1)}, bf16[32,1,1024]{2,0,1:T(8,128)(2,1)S(1)}, u32[]{:S(2)}) copy-start(bf16[32,1,1024]{2,0,1:T(8,128)(2,1)S(1)} %get-tuple-element.42) | copy-start | bytes 196612
  340.3 34.7 %copy-start.28 = (bf16[32,8,128,1]{2,1,0,3:T(8,128)(2,1)S(1)}, bf16[32,8,128,1]{2,1,0,3:T(8,128)(2,1)}, u32[]{:S(2)}) copy-start(bf16[32,8,128,1]{2,1,0,3:T(8,128)(2,1)} %copy-done.27) | copy-start | bytes 196612
  375.9 5.8 copy-start.22
  377.3 7.2 %copy-start.21 = (f32[32,1,8,128]{3,2,0,1:T(8,128)S(1)}, f32[32,1,8,128]{3,2,0,1:T(8,128)}, u32[]{:S(2)}) copy-start(f32[32,1,8,128]{3,2,0,1:T(8,128)} %get-tuple-element.69) | copy-start | bytes 393220
  380.9 6.6 copy-start.20
  382.7 6.0 copy-start.31
  382.7 6.7 %copy-start.19 = (f32[32,1,8,128]{3,2,0,1:T(8,128)S(1)}, f32[32,1,8,128]{3,2,0,1:T(8,128)}, u32[]{:S(2)}) copy-start(f32[32,1,8,128]{3,2,0,1:T(8,128)} %get-tuple-element.71) | copy-start | bytes 393220
  386.6 68.2 %copy-start.1 = (bf16[128,4096]{1,0:T(8,128)(2,1)S(1)}, bf16[128,4096]{1,0:T(8,128)(2,1)}, u32[]{:S(2)}) copy-start(bf16[128,4096]{1,0:T(8,128)(2,1)} %param.19) | copy-start | bytes 3145732
  390.4 239.9 %all-reduce.16.cloned.1.call-start = ((), (), s32[]{:S(2)}) async-start(), calls=%async_computation | async-start | bytes 8388608 | tf_op jit(solution)/shard_map/psum | solution.py:151
  407.7 48.3 %copy-start.16 = (f32[32,1,128]{2,0,1:T(8,128)S(1)}, f32[32,1,128]{2,0,1:T(8,128)}, u32[]{:S(2)}) copy-start(f32[32,1,128]{2,0,1:T(8,128)} %get-tuple-element.85) | copy-start | bytes 49156
  462.8 190.2 %all-reduce.22.cloned.1.call-start = ((), (), s32[]{:S(2)}) async-start(), calls=%async_computation.3 | async-start | bytes 131072 | tf_op jit(solution)/shard_map/psum | solution.py:156
  469.0 163.9 %copy-start.39 = (bf16[4096,128]{1,0:T(8,128)(2,1)S(1)}, bf16[4096,128]{1,0:T(8,128)(2,1)}, u32[]{:S(2)}) copy-start(bf16[4096,128]{1,0:T(8,128)(2,1)} %param.21) | copy-start | bytes 3145732
  636.0 16.9 %copy-start.18 = (f32[32,1,128]{2,0,1:T(8,128)S(1)}, f32[32,1,128]{2,0,1:T(8,128)}, u32[]{:S(2)}) copy-start(f32[32,1,128]{2,0,1:T(8,128)} %get-tuple-element.84) | copy-start | bytes 49156
  636.1 17.6 %copy-start.17 = (f32[32,1,128]{2,0,1:T(8,128)S(1)}, f32[32,1,128]{2,0,1:T(8,128)}, u32[]{:S(2)}) copy-start(f32[32,1,128]{2,0,1:T(8,128)} %get-tuple-element.85) | copy-start | bytes 49156
  (27 other events, 73.5 us)
Sparse Core Ops, SparseCore 0:
  58.7 105.0 all-reduce.19
  258.2 111.8 all-reduce.17
  390.5 17.0 all-reduce.23
  462.9 167.3 all-reduce.15
  636.1 16.7 all-reduce.21
where the time goes:
time: 665 us; the launch traced here: 663 us
  waiting for transfers between devices  322 us (48%)
  blocking collectives  242 us (36%)
  matrix products  47.1 us (7%)
  other arithmetic  25.5 us (4%)
  between operations  14.6 us (2%)
  local copies, waits for them, and re-layouts  11.3 us (2%)
    psum x1, waiting for transfers between devices, body(): gate_full, up_full = lax.psum((gate_part, up_part), 'seq')  161 us
    psum x2, waiting for transfers between devices, body(): lax.psum((query_part, key_part, value_part), 'seq')  130 us
    psum x1, blocking collectives, body(): lax.psum((query_part, key_part, value_part), 'seq')  81.7 us
    pmax x1, blocking collectives, body(): top_cache = lax.pmax(top_old, 'seq')  75.1 us
    psum x1, blocking collectives, body(): lax.psum((jnp.sum(widened, axis=-1), jnp.sum(widened * widened, axis=-1))...  43.5 us
    psum x1, blocking collectives, body(): lax.psum((jnp.sum(mixed, axis=-1), jnp.sum(mixed * mixed, axis=-1)), 'seq')  42 us
    psum x1, waiting for transfers between devices, body(): mixed = widened + lax.psum(attn_part, 'mdl')  17.2 us
  transfers between devices with their start and end apart: 5, of which 5 were waited for; matrix products, arithmetic and copies ran while one was open for 2% of the time, Pallas kernels for 0%

commit v1 on v0

--- a/solution.py
+++ b/solution.py
@@ -139,7 +139,7 @@
         attn_part = jnp.einsum(
             "rnm,mc->rnc", attended, out_weight, preferred_element_type=jnp.float32
         )
-        mixed = widened + lax.psum(attn_part, "mdl")
+        mixed = widened + jnp.sum(lax.all_gather(attn_part, "mdl"), axis=0)
         sums_mixed, squares_mixed = lax.psum(
             (jnp.sum(mixed, axis=-1), jnp.sum(mixed * mixed, axis=-1)), "seq"
         )

time: 665 us -> 645 us (0.970)
  waiting for transfers between devices: 322 us -> 304 us
    psum x1 -> x0, waiting for transfers between devices: 17.2 us -> none  [body(): mixed = widened + lax.psum(attn_part, 'mdl')]
    all_gather x0 -> x4, blocking collectives: none -> 7.34 us  [body(): mixed = widened + jnp.sum(lax.all_gather(attn_part, 'mdl'), axis=0)]
  transfers between devices with their start and end apart: 5 -> 4, of which waited for: 5 -> 4; matrix products, arithmetic and copies ran while one was open for 2% -> 2% of each run, Pallas kernels for 0% -> 0%
where the time goes in v1:
time: 645 us; the launch traced here: 644 us
  waiting for transfers between devices  304 us (47%)
  blocking collectives  248 us (38%)
  matrix products  44.7 us (7%)
  other arithmetic  21 us (3%)
  between operations  14.7 us (2%)
  local copies, waits for them, and re-layouts  11.2 us (2%)
    psum x1, waiting for transfers between devices, body(): gate_full, up_full = lax.psum((gate_part, up_part), 'seq')  160 us
    psum x2, waiting for transfers between devices, body(): lax.psum((query_part, key_part, value_part), 'seq')  130 us
    psum x1, blocking collectives, body(): lax.psum((query_part, key_part, value_part), 'seq')  81.7 us
    pmax x1, blocking collectives, body(): top_cache = lax.pmax(top_old, 'seq')  75.1 us
    psum x1, blocking collectives, body(): lax.psum((jnp.sum(widened, axis=-1), jnp.sum(widened * widened, axis=-1))...  43.5 us
    psum x1, blocking collectives, body(): lax.psum((jnp.sum(mixed, axis=-1), jnp.sum(mixed * mixed, axis=-1)), 'seq')  40.1 us
    psum x1, waiting for transfers between devices, body(): block_out = (mixed + lax.psum(down_part, 'mdl')).astype(jnp.bfloat16)  13.2 us
  transfers between devices with their start and end apart: 4, of which 4 were waited for; matrix products, arithmetic and copies ran while one was open for 2% of the time, Pallas kernels for 0%

profile of v1, /device:TPU:0, one launch (start us, length us, event | category | flops | bytes accessed | tf_op | source)
XLA Modules:
  0.0 643.6 jit_solution(15725568454562260478)
XLA Ops:
  8.5 43.5 %all-reduce.2 = (f32[32,1]{0,1:T(1,128)S(1)}, f32[32,1]{0,1:T(1,128)S(1)}, f32[32,1]{0,1:T(1,128)S(1)}, f32[32,1]{0,1:T(1,128)S(1)}, f32[32,1]{0,1:T(1,128)S(1)}...) all-reduce(f32[32,1]{0,1:T(1,128)S(1)} %bitcast.680, ...), channel_id=1, replica_groups=mesh['seq'=16,'mdl'=2] {'seq'}, use_global_device_ids=true, to_apply=%region_67.68 | all-reduce | flops 256 | bytes 2048 | tf_op jit(solution)/shard_map/psum | solution.py:70
  53.9 1.2 convolution_bitcast_fusion.19
  63.4 100.4 %all-reduce.18.cloned.1.call-done = (f32[32,1,8,128]{3,2,0,1:T(8,128)}, f32[32,1,8,128]{3,2,0,1:T(8,128)}, f32[32,1,8,128]{3,2,0,1:T(8,128)}, f32[32,1,8,128]{3,2,0,1:T(8,128)}) async-done(((f32[32,1,8,128]{3,2,0,1:T(8,128)}, f32[32,1,8,128]{3,2,0,1:T(8,128)}, f32[32,1,8,128]{3,2,0,1:T(8,128)}, f32[32,1,8,128]{3,2,0,1:T(8,128)}), (f32[32,1,8,128]{3,2,0,1:T(8,128)}, f32[32,1,8,128]{3,2,0,1:T(8,128)}, ...) | async-done | bytes 524304 | tf_op jit(solution)/shard_map/psum | solution.py:81
  163.8 1.2 fusion.71
  165.2 2.8 fusion.14
  168.2 1.2 fusion.12
  172.9 1.8 fusion
  174.6 1.8 fusion.2
  176.4 1.8 fusion.4
  178.2 1.8 fusion.6
  179.9 75.1 %all-reduce.6 = (f32[32,1,8]{2,0,1:T(8,128)S(1)}, f32[32,1,8]{2,0,1:T(8,128)S(1)}, f32[32,1,8]{2,0,1:T(8,128)S(1)}, f32[32,1,8]{2,0,1:T(8,128)S(1)}) all-reduce(f32[32,1,8]{2,0,1:T(8,128)S(1)} %bitcast.655, f32[32,1,8]{2,0,1:T(8,128)S(1)} %bitcast.654, f32[32,1,8]{2,0,1:T(8,128)S(1)} %bitcast.653, ...), channel_id=1, replica_groups=mesh['seq'=16,'mdl'=2] {'seq'}, use_global_device_ids=true, to_apply=%region_70.71 | all-reduce | flops 1024 | bytes 8192 | tf_op jit(solution)/shard_map/pmax | solution.py:107
  258.4 81.7 %all-reduce.21 = (bf16[32,1,1024]{2,0,1:T(8,128)(2,1)S(1)}, bf16[32,1,1024]{2,0,1:T(8,128)(2,1)S(1)}, bf16[32,1,1024]{2,0,1:T(8,128)(2,1)S(1)}, bf16[32,1,1024]{...) all-reduce(f32[32,1,1024]{2,0,1:T(8,128)S(1)} %convolution_bitcast_, ...), channel_id=1, replica_groups=mesh['seq'=16,'mdl'=2] {'seq'}, use_global_device_ids=true, to_apply=%region_74.75 | all-reduce | flops 132096 | bytes 794624 | tf_op jit(solution)/shard_map/psum | solution.py:81
  340.4 29.7 %all-reduce.16.cloned.1.call-done = (f32[32,1,8,128]{3,2,0,1:T(8,128)}, f32[32,1,8,128]{3,2,0,1:T(8,128)}, f32[32,1,8,128]{3,2,0,1:T(8,128)}, f32[32,1,8,128]{3,...) async-done(((f32[32,1,8,128]{3,2,0,1:T(8,128)}, f32[32,1,8,128]{3,2,0,1:T(8,128)}, ...) | async-done | bytes 1048592 | tf_op jit(solution)/shard_map/psum | solution.py:81
  379.8 1.8 all-gather.3
  383.9 1.8 all-gather.2
  388.9 1.8 all-gather.1
  392.2 1.8 all-gather
  394.2 40.1 %all-reduce = (f32[32,1]{0,1:T(1,128)S(1)}, f32[32,1]{0,1:T(1,128)S(1)}, f32[32,1]{0,1:T(1,128)S(1)}, f32[32,1]{0,1:T(1,128)S(1)}, f32[32,1]{0,1:T(1,128)S(1)}, ...) all-reduce(f32[32,1]{0,1:T(1,128)} %bitcast.688, ...), channel_id=1, replica_groups=mesh['seq'=16,'mdl'=2] {'seq'}, use_global_device_ids=true, to_apply=%region_82.83 | all-reduce | flops 256 | bytes 2048 | tf_op jit(solution)/shard_map/psum | solution.py:143
  443.6 1.5 copy.42
  446.9 3.4 convert_select_fusion
  450.4 160.4 %all-reduce.14.cloned.1.call-done = (f32[32,1,4096]{2,0,1:T(8,128)}, f32[32,1,4096]{2,0,1:T(8,128)}, f32[32,1,4096]{2,0,1:T(8,128)}, f32[32,1,4096]{2,0,1:T(8,12...) async-done(((f32[32,1,4096]{2,0,1:T(8,128)}, f32[32,1,4096]{2,0,1:T(8,128)}, f32[32,1,4096]{2,0,1:T(8,128)}, ...) | async-done | bytes 4194320 | tf_op jit(solution)/shard_map/psum | solution.py:151
  610.9 2.6 convolution_bitcast_fusion.20
  616.6 3.7 convert_select_fusion.1
  620.3 13.2 %all-reduce.20.cloned.1.call-done = (f32[32,1,128]{2,0,1:T(8,128)}, f32[32,1,128]{2,0,1:T(8,128)}, f32[32,1,128]{2,0,1:T(8,128)}, f32[32,1,128]{2,0,1:T(8,128)}) async-done(((f32[32,1,128]{2,0,1:T(8,128)}, f32[32,1,128]{2,0,1:T(8,128)}, f32[32,1,128]{2,0,1:T(8,128)}, f32[32,1,128]{2,0,1:T(8,128)}), (f32[32,1,128]{2,0,1:T(8,128)}, f32[32,1,128]{2,0,1:T(8,128)}, f32[32,1,128]{2,0,1:T(8,128)}, ...) | async-done | bytes 65552 | tf_op jit(solution)/shard_map/psum | solution.py:156
  (253 shorter events, 52.8 us)
Async XLA Ops:
  7.2 427.2 %copy-start = (bf16[128,4096]{1,0:T(8,128)(2,1)S(1)}, bf16[128,4096]{1,0:T(8,128)(2,1)}, u32[]{:S(2)}) copy-start(bf16[128,4096]{1,0:T(8,128)(2,1)} %param.20) | copy-start | bytes 3145732
  7.2 50.5 %copy-start.2 = (bf16[128,1024]{1,0:T(8,128)(2,1)S(1)}, bf16[128,1024]{1,0:T(8,128)(2,1)}, u32[]{:S(2)}) copy-start(bf16[128,1024]{1,0:T(8,128)(2,1)} %param.15) | copy-start | bytes 786436
  7.2 51.5 %copy-start.3 = (bf16[128,1024]{1,0:T(8,128)(2,1)S(1)}, bf16[128,1024]{1,0:T(8,128)(2,1)}, u32[]{:S(2)}) copy-start(bf16[128,1024]{1,0:T(8,128)(2,1)} %param.16) | copy-start | bytes 786436
  7.2 156.6 %all-reduce.18.cloned.1.call-start = ((), (), s32[]{:S(2)}) async-start(), calls=%async_computation.2 | async-start | bytes 1048576 | tf_op jit(solution)/shard_map/psum | solution.py:81
  53.9 5.7 copy-start.4
  58.6 311.5 %all-reduce.16.cloned.1.call-start = ((), (), s32[]{:S(2)}) async-start(), calls=%async_computation.1 | async-start | bytes 2097152 | tf_op jit(solution)/shard_map/psum | solution.py:81
  62.9 102.1 %copy-start.29 = (s32[32,4]{0,1:T(4,128)}, s32[32,4]{0,1:T(4,128)S(1)}, u32[]{:S(2)}) copy-start(s32[32,4]{0,1:T(4,128)S(1)} %iota_add_fusion) | copy-start | bytes 1540
  63.0 102.1 %copy-start.34 = (s32[32]{0:T(128)}, s32[32]{0:T(128)S(1)}, u32[]{:S(2)}) copy-start(s32[32]{0:T(128)S(1)} %iota_add_fusion.1) | copy-start | bytes 388
  258.1 352.7 %all-reduce.14.cloned.1.call-start = ((), (), s32[]{:S(2)}) async-start(), calls=%async_computation | async-start | bytes 8388608 | tf_op jit(solution)/shard_map/psum | solution.py:151
  340.1 34.7 %copy-start.13 = (bf16[32,1,1024]{2,0,1:T(8,128)(2,1)}, bf16[32,1,1024]{2,0,1:T(8,128)(2,1)S(1)}, u32[]{:S(2)}) copy-start(bf16[32,1,1024]{2,0,1:T(8,128)(2,1)S(1)} %get-tuple-element.40) | copy-start | bytes 196612
  340.2 34.7 %copy-start.14 = (bf16[32,1,1024]{2,0,1:T(8,128)(2,1)}, bf16[32,1,1024]{2,0,1:T(8,128)(2,1)S(1)}, u32[]{:S(2)}) copy-start(bf16[32,1,1024]{2,0,1:T(8,128)(2,1)S(1)} %get-tuple-element.41) | copy-start | bytes 196612
  340.2 43.4 %copy-start.15 = (bf16[32,1,1024]{2,0,1:T(8,128)(2,1)}, bf16[32,1,1024]{2,0,1:T(8,128)(2,1)S(1)}, u32[]{:S(2)}) copy-start(bf16[32,1,1024]{2,0,1:T(8,128)(2,1)S(1)} %get-tuple-element.42) | copy-start | bytes 196612
  340.3 34.7 %copy-start.26 = (bf16[32,8,128,1]{2,1,0,3:T(8,128)(2,1)S(1)}, bf16[32,8,128,1]{2,1,0,3:T(8,128)(2,1)}, u32[]{:S(2)}) copy-start(bf16[32,8,128,1]{2,1,0,3:T(8,128)(2,1)} %copy-done.25) | copy-start | bytes 196612
  376.7 6.8 %copy-start.30 = (f32[32,1,8]{2,0,1:T(8,128)S(1)}, f32[32,1,8]{2,0,1:T(8,128)}, u32[]{:S(2)}) copy-start(f32[32,1,8]{2,0,1:T(8,128)} %get-tuple-element.45) | copy-start | bytes 3076
  377.1 6.4 %copy-start.19 = (f32[32,1,8,128]{3,2,0,1:T(8,128)S(1)}, f32[32,1,8,128]{3,2,0,1:T(8,128)}, u32[]{:S(2)}) copy-start(f32[32,1,8,128]{3,2,0,1:T(8,128)} %get-tuple-element.69) | copy-start | bytes 393220
  379.4 8.3 %copy-start.27 = (f32[32,8]{1,0:T(8,128)S(1)}, f32[32,8]{1,0:T(8,128)}, u32[]{:S(2)}) copy-start(f32[32,8]{1,0:T(8,128)} %copy.34) | copy-start | bytes 3076
  379.4 9.1 %copy-start.18 = (f32[32,1,8,128]{3,2,0,1:T(8,128)S(1)}, f32[32,1,8,128]{3,2,0,1:T(8,128)}, u32[]{:S(2)}) copy-start(f32[32,1,8,128]{3,2,0,1:T(8,128)} %get-tuple-element.70) | copy-start | bytes 393220
  382.5 9.3 %copy-start.17 = (f32[32,1,8,128]{3,2,0,1:T(8,128)S(1)}, f32[32,1,8,128]{3,2,0,1:T(8,128)}, u32[]{:S(2)}) copy-start(f32[32,1,8,128]{3,2,0,1:T(8,128)} %get-tuple-element.71) | copy-start | bytes 393220
  387.7 47.8 %copy-start.1 = (bf16[128,4096]{1,0:T(8,128)(2,1)S(1)}, bf16[128,4096]{1,0:T(8,128)(2,1)}, u32[]{:S(2)}) copy-start(bf16[128,4096]{1,0:T(8,128)(2,1)} %param.19) | copy-start | bytes 3145732
  388.5 5.6 copy-start.37
  394.0 47.0 %copy-start.11 = (f32[32,128]{1,0:T(8,128)}, f32[32,128]{1,0:T(8,128)S(1)}, u32[]{:S(2)}) copy-start(f32[32,128]{1,0:T(8,128)S(1)} %reduce.48) | copy-start | bytes 49156
  443.3 190.2 %all-reduce.20.cloned.1.call-start = ((), (), s32[]{:S(2)}) async-start(), calls=%async_computation.3 | async-start | bytes 131072 | tf_op jit(solution)/shard_map/psum | solution.py:156
  450.3 163.1 %copy-start.40 = (bf16[4096,128]{1,0:T(8,128)(2,1)S(1)}, bf16[4096,128]{1,0:T(8,128)(2,1)}, u32[]{:S(2)}) copy-start(bf16[4096,128]{1,0:T(8,128)(2,1)} %param.21) | copy-start | bytes 3145732
  616.6 19.1 %copy-start.12 = (f32[32,128]{1,0:T(8,128)S(1)}, f32[32,128]{1,0:T(8,128)}, u32[]{:S(2)}) copy-start(f32[32,128]{1,0:T(8,128)} %copy-done.11) | copy-start | bytes 49156
  (27 other events, 66.5 us)
Sparse Core Ops, SparseCore 0:
  58.7 105.0 all-reduce.17
  258.2 111.8 all-reduce.15
  443.5 167.3 all-reduce.13
  616.7 16.7 all-reduce.19
